TPU v7x, 32 devices: a whole 2x2x4 slice. The times are simulated.
32 devices in a mesh: ctx: 4 (over z), dom: 2 (over y), rep: 4 (over x, core).
Axes of the slice: x: 2, y: 2, z: 4, core: 2. Of those that a mesh axis runs over, the one named last changes fastest.
Arguments:
- hidden: bfloat16 [4, 2, 512, 2048], P('rep', 'dom', 'ctx'), may hold values from -6 to 6
- bmat: bfloat16 [4, 2, 512, 128], P('rep', 'dom', 'ctx'), may hold values from -0.5 to 0.5
- cmat: bfloat16 [4, 2, 512, 128], P('rep', 'dom', 'ctx'), may hold values from -6 to 6
- tokens: int32 [4, 2, 512], P('rep', 'dom', 'ctx'), may hold values from 0 to 3
- table: float32 [4, 128], replicated, may hold values from -0.5 to 0.5
- step_size: float32 [4, 2, 512, 16], P('rep', 'dom', 'ctx'), may hold values from 0.005 to 0.05
- log_decay: float32 [4, 2, 512, 16], P('rep', 'dom', 'ctx'), may hold values from 0 to 1.5
- skip_gain: float32 [16], replicated, may hold values from 0.5 to 1.5
- prev_state: float32 [4, 2, 16, 128, 128], P('rep', 'dom', 'ctx'), may hold values from -0.5 to 0.5
- ancestors: int32 [4, 2], P('rep', 'dom'), may hold values from 0 to 1
- suffix_start: int32 [4], P('rep'), may hold values from 128 to 511
- cotangent: bfloat16 [4, 2, 512, 2048], P('rep', 'dom', 'ctx'), may hold values from -6 to 6
Outputs:
- mixed: bfloat16 [4, 2, 512, 2048], P('rep', 'dom', 'ctx')
- grad_hidden: bfloat16 [4, 2, 512, 2048], P('rep', 'dom', 'ctx')
- grad_bmat: bfloat16 [4, 2, 512, 128], P('rep', 'dom', 'ctx')
- grad_cmat: bfloat16 [4, 2, 512, 128], P('rep', 'dom', 'ctx')
- grad_table: float32 [4, 128], replicated
- grad_skip: float32 [16], replicated
All inputs are finite; a program needn't handle non-finite values.
Results may differ from a plain program's by a relative error of at most 0.008.
Values sent between devices are 32-bit elements; how exact they have to be, the bound alone decides.
No kernel may reach another device: no remote copies, remote signals or barrier semaphores. Data moves between devices by JAX's collectives and lax.ppermute only.
A program may use at most 192 MiB of HBM per device.

v0:
```python
import math
import jax
import jax.numpy as jnp
from jax import lax
from jax.sharding import PartitionSpec as P


def carried_in(value, axis, join, neutral, backward):
    count, mine = (lax.axis_size(axis), lax.axis_index(axis))
    pieces = jax.tree.map(lambda part: lax.all_gather(part, axis), value)
    if backward:
        pieces = jax.tree.map(lambda part: part[::-1], pieces)
        mine = count - 1 - mine
    running = jax.tree.map(
        lambda part, zero: jnp.full_like(part, 0) + jnp.asarray(zero, part.dtype), value, neutral
    )

    def turn(position, running):
        longer = join(running, jax.tree.map(lambda part: part[position], pieces))
        return jax.tree.map(lambda new, old: jnp.where(position < mine, new, old), longer, running)

    return lax.fori_loop(0, count - 1, turn, running)


def weigh(factor, values):
    return (factor[:, :, None] * values.astype(jnp.float32)).astype(jnp.bfloat16)


def block_terms(hidden_rows, writer, reader, step_rows, rate_rows, grad_rows):
    cumulative = jnp.cumsum(rate_rows, axis=0)
    totals = cumulative[-1]
    scaled = (step_rows[:, :, None] * hidden_rows.astype(jnp.float32)).astype(jnp.bfloat16)
    inner_dot = jnp.einsum("tn,sn->ts", reader, writer, preferred_element_type=jnp.float32)
    across = cumulative.T
    kernel = jnp.exp(-jnp.abs(across[:, :, None] - across[:, None, :]))
    weights = (kernel * inner_dot[None]).astype(jnp.bfloat16)
    mixed_in = jnp.einsum("hts,shp->thp", weights, scaled, preferred_element_type=jnp.float32)
    back_in = jnp.einsum("hts,thp->shp", weights, grad_rows, preferred_element_type=jnp.float32)
    paired = jnp.einsum("thp,shp->hts", grad_rows, scaled, preferred_element_type=jnp.float32)
    crossed = jnp.sum(kernel * paired, axis=0).astype(jnp.bfloat16)
    reader_in = jnp.einsum("ts,sn->tn", crossed, writer, preferred_element_type=jnp.float32)
    writer_in = jnp.einsum("ts,tn->sn", crossed, reader, preferred_element_type=jnp.float32)
    rising = jnp.exp(-cumulative)
    falling = jnp.exp(-(totals[None] - cumulative))
    state_end = jnp.einsum(
        "shp,sn->hpn", weigh(falling, scaled), writer, preferred_element_type=jnp.float32
    )
    state_begin = jnp.einsum(
        "shp,sn->hpn", weigh(rising, scaled), writer, preferred_element_type=jnp.float32
    )
    grad_end = jnp.einsum(
        "thp,tn->hpn", weigh(falling, grad_rows), reader, preferred_element_type=jnp.float32
    )
    grad_begin = jnp.einsum(
        "thp,tn->hpn", weigh(rising, grad_rows), reader, preferred_element_type=jnp.float32
    )
    decays = jnp.exp(-totals)
    return (
        mixed_in,
        back_in,
        reader_in,
        writer_in,
        rising,
        falling,
        scaled,
        decays,
        state_end,
        state_begin,
        grad_end,
        grad_begin,
    )


def finish(
    hidden_rows,
    writer,
    reader,
    step_rows,
    grad_rows,
    skip_gain,
    block_out,
    state_in,
    state_back,
    grad_in,
    grad_back,
):
    mixed_in, back_in, reader_in, writer_in, rising, falling, scaled = block_out
    state_in = state_in.astype(jnp.bfloat16)
    state_back = state_back.astype(jnp.bfloat16)
    grad_in = grad_in.astype(jnp.bfloat16)
    grad_back = grad_back.astype(jnp.bfloat16)
    rise = rising[:, :, None]
    fall = falling[:, :, None]
    mixed = (
        mixed_in
        + rise * jnp.einsum("hpn,tn->thp", state_in, reader, preferred_element_type=jnp.float32)
        + fall * jnp.einsum("hpn,tn->thp", state_back, reader, preferred_element_type=jnp.float32)
        + skip_gain[None, :, None] * hidden_rows.astype(jnp.float32)
    )
    back = (
        back_in
        + rise * jnp.einsum("hpn,sn->shp", grad_in, writer, preferred_element_type=jnp.float32)
        + fall * jnp.einsum("hpn,sn->shp", grad_back, writer, preferred_element_type=jnp.float32)
    )
    grad_hidden = step_rows[:, :, None] * back + skip_gain[None, :, None] * grad_rows.astype(
        jnp.float32
    )
    grad_reader = reader_in + jnp.sum(
        rise * jnp.einsum("thp,hpn->thn", grad_rows, state_in, preferred_element_type=jnp.float32)
        + fall
        * jnp.einsum("thp,hpn->thn", grad_rows, state_back, preferred_element_type=jnp.float32),
        axis=1,
    )
    grad_writer = writer_in + jnp.sum(
        rise * jnp.einsum("shp,hpn->shn", scaled, grad_in, preferred_element_type=jnp.float32)
        + fall * jnp.einsum("shp,hpn->shn", scaled, grad_back, preferred_element_type=jnp.float32),
        axis=1,
    )
    return (
        mixed.astype(jnp.bfloat16),
        grad_hidden.astype(jnp.bfloat16),
        grad_reader.astype(jnp.bfloat16),
        grad_writer,
    )


def chain_pair(earlier, latter):
    return (earlier[0] * latter[0], earlier[1] * latter[0][:, :, None, None] + latter[1])


def per_device(
    hidden,
    bmat,
    cmat,
    tokens,
    table,
    step_size,
    log_decay,
    skip_gain,
    prev_state,
    ancestors,
    suffix_start,
    cotangent,
):
    prompt_count, part_count, length, feature_dim = hidden.shape
    pair_count = prompt_count * part_count
    head_count = skip_gain.shape[0]
    head_dim = feature_dim // head_count
    state_dim = bmat.shape[3]
    vocab_size = table.shape[0]
    onehot = (tokens[..., None] == jnp.arange(vocab_size)[None, None, None, :]).astype(jnp.float32)
    looked = jnp.einsum("rplv,vn->rpln", onehot, table, precision=lax.Precision.HIGHEST)
    writer_all = (bmat.astype(jnp.float32) + looked).astype(jnp.bfloat16)
    symbol_site_indices = lax.axis_index("ctx") * length + jnp.arange(length)
    live_rows = symbol_site_indices[None, :] < suffix_start[:, None]
    grad_all = jnp.where(live_rows[:, None, :, None], cotangent, jnp.zeros_like(cotangent))
    shard_part = lax.all_gather(prev_state, "dom", axis=1, tiled=True)
    owners = jnp.arange(shard_part.shape[1])
    chosen = (ancestors[:, :, None] == owners[None, None, :]).astype(jnp.float32)
    chosen_heads = jnp.einsum(
        "rpk,rkhdn->rphdn", chosen, shard_part, precision=lax.Precision.HIGHEST
    )
    begin_state = lax.all_gather(chosen_heads, "ctx", axis=2, tiled=True).reshape(
        pair_count, head_count, head_dim, state_dim
    )
    hidden_rows = hidden.reshape(pair_count, length, head_count, head_dim)
    grad_rows = grad_all.reshape(pair_count, length, head_count, head_dim)
    writer = writer_all.reshape(pair_count, length, state_dim)
    reader = cmat.reshape(pair_count, length, state_dim)
    step_rows = step_size.reshape(pair_count, length, head_count)
    rate_rows = log_decay.reshape(pair_count, length, head_count)
    block_out = jax.vmap(block_terms)(hidden_rows, writer, reader, step_rows, rate_rows, grad_rows)
    decays, state_end, state_begin, grad_end, grad_begin = block_out[7:]
    at_first = jnp.where(lax.axis_index("ctx") == 0, 1.0, 0.0)
    seeded = state_end + at_first * decays[:, :, None, None] * begin_state
    unit_decay = jnp.ones_like(decays)
    zero_state = jnp.zeros_like(state_end)
    state_in = carried_in((decays, seeded), "ctx", chain_pair, (unit_decay, zero_state), False)[1]
    state_back = carried_in(
        (decays, state_begin), "ctx", chain_pair, (unit_decay, zero_state), True
    )[1]
    grad_in = carried_in((decays, grad_end), "ctx", chain_pair, (unit_decay, zero_state), False)[1]
    grad_back = carried_in((decays, grad_begin), "ctx", chain_pair, (unit_decay, zero_state), True)[
        1
    ]
    state_in = state_in + at_first * begin_state
    results = jax.vmap(finish, in_axes=(0, 0, 0, 0, 0, None, 0, 0, 0, 0, 0))(
        hidden_rows,
        writer,
        reader,
        step_rows,
        grad_rows,
        skip_gain,
        block_out[:7],
        state_in,
        state_back,
        grad_in,
        grad_back,
    )
    mixed = results[0].reshape(hidden.shape)
    grad_hidden = results[1].reshape(hidden.shape)
    grad_cmat = results[2].reshape(cmat.shape)
    grad_writer = results[3]
    total_rows = (
        pair_count * length * lax.axis_size("ctx") * lax.axis_size("dom") * lax.axis_size("rep")
    )
    writer_scale = 1.0 / math.sqrt(head_count * head_dim)
    total_scale = 1.0 / math.sqrt(total_rows)
    grad_bmat = (grad_writer * writer_scale).astype(jnp.bfloat16).reshape(bmat.shape)
    table_part = jnp.einsum(
        "clv,cln->vn",
        onehot.reshape(pair_count, length, vocab_size),
        grad_writer,
        precision=lax.Precision.HIGHEST,
    ) * (writer_scale * total_scale)
    skip_part = jnp.einsum(
        "clhp,clhp->h", hidden_rows, grad_rows, preferred_element_type=jnp.float32
    ) * (total_scale / math.sqrt(head_dim))
    grad_table, grad_skip = lax.psum((table_part, skip_part), ("ctx", "dom", "rep"))
    return (mixed, grad_hidden, grad_bmat, grad_cmat, grad_table, grad_skip)


def solution(mesh):
    return jax.shard_map(
        per_device,
        mesh=mesh,
        in_specs=(
            P("rep", "dom", "ctx", None),
            P("rep", "dom", "ctx", None),
            P("rep", "dom", "ctx", None),
            P("rep", "dom", "ctx"),
            P(),
            P("rep", "dom", "ctx", None),
            P("rep", "dom", "ctx", None),
            P(),
            P("rep", "dom", "ctx", None, None),
            P("rep", "dom"),
            P("rep"),
            P("rep", "dom", "ctx", None),
        ),
        out_specs=(
            P("rep", "dom", "ctx", None),
            P("rep", "dom", "ctx", None),
            P("rep", "dom", "ctx", None),
            P("rep", "dom", "ctx", None),
            P(),
            P(),
        ),
        check_vma=False,
    )
```

profile of v0, /device:TPU:0, one launch (start us, length us, event | category | flops | bytes accessed | tf_op | source)
XLA Modules:
  0.0 392.6 jit_solution(15929040369824743849)
XLA Ops:
  7.2 10.2 %all_gather.41 = f32[1,2,4,128,128]{4,3,2,0,1:T(8,128)S(1)} all-gather(f32[1,1,4,128,128]{4,3,2,0,1:T(8,128)} %bitcast.289), channel_id=1, replica_groups=mesh['ctx'=4,'dom'=2,'rep'=4] {'dom'}, dimensions={1}, use_global_device_ids=true | all-gather | bytes 786432 | tf_op jit(solution)/shard_map/all_gather | solution.py:157
  18.1 2.0 fusion.43
  22.8 1.6 copy.99
  24.5 1.3 mul.337.clone
  25.8 2.4 mul.344
  28.9 3.0 fusion.32
  31.9 1.4 copy.141
  33.5 1.3 fusion.64
  34.9 1.3 copy.143
  37.8 1.3 fusion.58
  41.1 8.6 %all-gather.11.cloned.1.call-done = f32[16,128,128]{2,1,0:T(8,128)} async-done(((f32[4,128,128]{2,1,0:T(8,128)}), f32[16,128,128]{2,1,0:T(8,128)}) %all-gather.11.cloned.1.call-update) | async-done | bytes 1048592 | tf_op jit(solution)/shard_map/all_gather | solution.py:163
  49.6 2.5 convolution_add_fusion
  52.5 2.2 copy.106
  54.8 9.5 %all_gather.40 = f32[4,1,16]{2,1,0:T(1,128)S(1)} all-gather(f32[1,1,16]{2,1,0:T(1,128)S(1)} %get-tuple-element.554), channel_id=1, replica_groups=mesh['ctx'=4,'dom'=2,'rep'=4] {'ctx'}, dimensions={0}, use_global_device_ids=true | all-gather | bytes 320 | tf_op jit(solution)/shard_map/all_gather | solution.py:10
  64.5 2.5 copy.114
  67.0 1.9 fusion.27
  68.9 62.6 %all-gather.15.cloned.1.call-done = f32[64,128,128]{2,1,0:T(8,128)} async-done(((f32[16,128,128]{2,1,0:T(8,128)}), f32[64,128,128]{2,1,0:T(8,128)}) %all-gather.15.cloned.1.call-update) | async-done | bytes 4194320 | tf_op jit(solution)/shard_map/all_gather | solution.py:10
  131.5 4.6 %rev.11 = f32[4,1,16,128,128]{4,3,2,1,0:T(8,128)} reverse(f32[4,1,16,128,128]{4,3,2,1,0:T(8,128)} %bitcast.277), dimensions={0} | reverse | bytes 8388608 | tf_op jit(solution)/shard_map/rev | solution.py:12
  136.1 76.3 %all-gather.19.cloned.1.call-done = f32[64,128,128]{2,1,0:T(8,128)} async-done(((f32[16,128,128]{2,1,0:T(8,128)}), f32[64,128,128]{2,1,0:T(8,128)}) %all-gather.19.cloned.1.call-update) | async-done | bytes 4194320 | tf_op jit(solution)/shard_map/all_gather | solution.py:10
  212.4 4.7 %rev.12 = f32[4,1,16,128,128]{4,3,2,1,0:T(8,128)} reverse(f32[4,1,16,128,128]{4,3,2,1,0:T(8,128)} %bitcast.278), dimensions={0} | reverse | bytes 8388608 | tf_op jit(solution)/shard_map/rev | solution.py:12
  217.0 4.6 %while.59 = (s32[]{:T(128)}, f32[1,16,128,128]{3,2,1,0:T(8,128)S(1)}, s32[]{:T(128)}, f32[4,1,16]{2,1,0:T(1,128)S(1)}, f32[4,1,16,128,128]{4,3,2,1,0:T(8,128)}, /*index=5*/s32[]{:T(128)}, s32[]{:T(128)}) while((s32[]{:T(128)}, f32[1,16,128,128]{3,2,1,0:T(8,128)S(1)}, s32[]{:T(128)}, f32[4,1,16]{2,1,0:T(1,128)S(1)}, ...), condition=%wide.region_8.9_spmd.clone, body=%wide.region_7.8_spmd.clone.sunk | while | flops 1048580 | bytes 3146025 | solution.py:22
  217.1 1.5 fusion.99
  218.5 1.6 fusion.99
  220.1 1.5 fusion.99
  221.7 1.3 fusion.8
  223.0 70.2 %all-gather.17.cloned.1.call-done = f32[64,128,128]{2,1,0:T(8,128)} async-done(((f32[16,128,128]{2,1,0:T(8,128)}), f32[64,128,128]{2,1,0:T(8,128)}) %all-gather.17.cloned.1.call-update) | async-done | bytes 4194320 | tf_op jit(solution)/shard_map/all_gather | solution.py:10
  293.1 4.5 %while.58 = (s32[]{:T(128)}, f32[1,16,128,128]{3,2,1,0:T(8,128)S(1)}, s32[]{:T(128)}, f32[4,1,16]{2,1,0:T(1,128)S(1)}, f32[4,1,16,128,128]{4,3,2,1,0:T(8,128)}, /*index=5*/s32[]{:T(128)}, s32[]{:T(128)}) while((s32[]{:T(128)}, f32[1,16,128,128]{3,2,1,0:T(8,128)S(1)}, s32[]{:T(128)}, f32[4,1,16]{2,1,0:T(1,128)S(1)}, ...), condition=%wide.region_6.7_spmd.clone, body=%wide.region_5.6_spmd.clone.sunk | while | flops 1048580 | bytes 3146025 | solution.py:22
  293.1 1.5 fusion.98
  294.6 1.5 fusion.98
  296.1 1.5 fusion.98
  297.9 3.4 fusion.23
  301.3 2.1 copy.125
  303.4 1.7 fusion.19
  305.1 1.8 fusion.26
  307.5 43.5 %all-reduce = (f32[4,128]{1,0:T(4,128)}, f32[16]{0:T(128)}) all-reduce(f32[4,128]{1,0:T(4,128)S(1)} %convolution_multiply_fusion.3, f32[16]{0:T(128)S(1)} %broadcast_multiply_fusion), channel_id=1, replica_groups=mesh['ctx'=4,'dom'=2,'rep'=4] {'ctx','dom','rep'}, use_global_device_ids=true, to_apply=%region_12.13 | all-reduce | flops 528 | bytes 4224 | tf_op jit(solution)/shard_map/psum | solution.py:219
  351.0 4.5 %while.57 = (s32[]{:T(128)}, f32[1,16,128,128]{3,2,1,0:T(8,128)S(1)}, s32[]{:T(128)}, f32[4,1,16]{2,1,0:T(1,128)S(1)}, f32[4,1,16,128,128]{4,3,2,1,0:T(8,128)}, /*index=5*/s32[]{:T(128)}, s32[]{:T(128)}) while((s32[]{:T(128)}, f32[1,16,128,128]{3,2,1,0:T(8,128)S(1)}, s32[]{:T(128)}, f32[4,1,16]{2,1,0:T(1,128)S(1)}, ...), condition=%wide.region_4.5_spmd.clone, body=%wide.region_3.4_spmd.clone.sunk | while | flops 1048580 | bytes 3146025 | solution.py:22
  351.0 1.5 fusion.97
  352.5 1.5 fusion.97
  354.0 1.5 fusion.97
  355.5 1.3 fusion.7
  357.4 1.5 fusion.22
  359.0 15.9 %all-gather.13.cloned.1.call-done = f32[64,128,128]{2,1,0:T(8,128)} async-done(((f32[16,128,128]{2,1,0:T(8,128)}), f32[64,128,128]{2,1,0:T(8,128)}) %all-gather.13.cloned.1.call-update) | async-done | bytes 4194320 | tf_op jit(solution)/shard_map/all_gather | solution.py:10
  374.9 4.5 %while.56 = (s32[]{:T(128)}, f32[1,16,128,128]{3,2,1,0:T(8,128)S(1)}, s32[]{:T(128)}, f32[4,1,16]{2,1,0:T(1,128)S(1)}, f32[4,1,16,128,128]{4,3,2,1,0:T(8,128)}, /*index=5*/s32[]{:T(128)}, s32[]{:T(128)}) while((s32[]{:T(128)}, f32[1,16,128,128]{3,2,1,0:T(8,128)S(1)}, s32[]{:T(128)}, f32[4,1,16]{2,1,0:T(1,128)S(1)}, ...), condition=%wide.region_2.3_spmd.clone, body=%wide.region_1.2_spmd.clone.sunk | while | flops 1048580 | bytes 3146025 | solution.py:22
  374.9 1.5 fusion.96
  376.4 1.5 fusion.96
  377.9 1.5 fusion.96
  379.4 1.5 fusion.36
  382.5 2.6 fusion.24
  (92 shorter events, 11.3 us)
Async XLA Ops:
  7.2 29.0 %copy-start = (bf16[1,1,128,128]{3,2,1,0:T(8,128)(2,1)S(1)}, bf16[1,1,128,128]{3,2,1,0:T(8,128)(2,1)}, u32[]{:S(2)}) copy-start(bf16[1,1,128,128]{3,2,1,0:T(8,128)(2,1)} %param.22) | copy-start | bytes 98308
  7.2 42.4 %all-gather.11.cloned.1.call-start = ((), (), s32[]{:S(2)}) async-start(), calls=%async_computation | async-start | bytes 1310720 | tf_op jit(solution)/shard_map/all_gather | solution.py:163
  7.2 17.1 %copy-start.11 = (f32[1,1,128,16]{2,3,1,0:T(8,128)S(1)}, f32[1,1,128,16]{2,3,1,0:T(8,128)}, u32[]{:S(2)}) copy-start(f32[1,1,128,16]{2,3,1,0:T(8,128)} %param.25) | copy-start | bytes 24580
  20.1 111.4 %all-gather.15.cloned.1.call-start = ((), (), s32[]{:S(2)}) async-start(), calls=%async_computation.2 | async-start | bytes 5242880 | tf_op jit(solution)/shard_map/all_gather | solution.py:10
  21.4 7.5 %copy-start.6 = (bf16[1,1,128,2048]{3,2,1,0:T(8,128)(2,1)S(1)}, bf16[1,1,128,2048]{3,2,1,0:T(8,128)(2,1)}, u32[]{:S(2)}) copy-start(bf16[1,1,128,2048]{3,2,1,0:T(8,128)(2,1)} %param.20) | copy-start | bytes 1572868
  21.4 7.5 %copy-start.8 = (bf16[1,1,128,2048]{3,2,1,0:T(8,128)(2,1)S(1)}, bf16[1,1,128,2048]{3,2,1,0:T(8,128)(2,1)}, u32[]{:S(2)}) copy-start(bf16[1,1,128,2048]{3,2,1,0:T(8,128)(2,1)} %param.31) | copy-start | bytes 1572868
  28.2 5.1 %copy-start.13 = (s32[1,1,128]{2,1,0:T(1,128)S(1)}, s32[1,1,128]{2,1,0:T(1,128)}, u32[]{:S(2)}) copy-start(s32[1,1,128]{2,1,0:T(1,128)} %param.23) | copy-start | bytes 1540
  28.2 5.1 %copy-start.14 = (bf16[1,1,128,128]{3,2,1,0:T(8,128)(2,1)S(1)}, bf16[1,1,128,128]{3,2,1,0:T(8,128)(2,1)}, u32[]{:S(2)}) copy-start(bf16[1,1,128,128]{3,2,1,0:T(8,128)(2,1)} %param.21) | copy-start | bytes 98308
  28.2 5.1 %copy-start.15 = (f32[4,128]{1,0:T(4,128)S(1)}, f32[4,128]{1,0:T(4,128)}, u32[]{:S(2)}) copy-start(f32[4,128]{1,0:T(4,128)} %param.24) | copy-start | bytes 6148
  31.9 5.7 %copy-start.10 = (bf16[1,1,128,2048]{3,2,1,0:T(8,128)(2,1)S(1)}, bf16[1,1,128,2048]{3,2,1,0:T(8,128)(2,1)}, u32[]{:S(2)}) copy-start(bf16[1,1,128,2048]{3,2,1,0:T(8,128)(2,1)} %get-tuple-element.551) | copy-start | bytes 1572868
  34.8 177.6 %all-gather.19.cloned.1.call-start = ((), (), s32[]{:S(2)}) async-start(), calls=%async_computation.4 | async-start | bytes 5242880 | tf_op jit(solution)/shard_map/all_gather | solution.py:10
  37.5 3.0 copy-start.9
  37.5 255.7 %all-gather.17.cloned.1.call-start = ((), (), s32[]{:S(2)}) async-start(), calls=%async_computation.3 | async-start | bytes 5242880 | tf_op jit(solution)/shard_map/all_gather | solution.py:10
  39.2 335.7 %all-gather.13.cloned.1.call-start = ((), (), s32[]{:S(2)}) async-start(), calls=%async_computation.1 | async-start | bytes 5242880 | tf_op jit(solution)/shard_map/all_gather | solution.py:10
  40.5 11.6 %copy-start.4 = (bf16[16,8,16,128]{3,2,1,0:T(8,128)(2,1)}, bf16[16,8,16,128]{3,2,1,0:T(8,128)(2,1)S(1)}, u32[]{:S(2)}) copy-start(bf16[16,8,16,128]{3,2,1,0:T(8,128)(2,1)S(1)} %copy.147) | copy-start | bytes 1572868
  40.9 11.2 %copy-start.2 = (bf16[16,8,16,128]{3,2,1,0:T(8,128)(2,1)}, bf16[16,8,16,128]{3,2,1,0:T(8,128)(2,1)S(1)}, u32[]{:S(2)}) copy-start(bf16[16,8,16,128]{3,2,1,0:T(8,128)(2,1)S(1)} %copy.146) | copy-start | bytes 1572868
  293.1 4.8 %copy-start.12 = (f32[16]{0:T(128)S(1)}, f32[16]{0:T(128)}, u32[]{:S(2)}) copy-start(f32[16]{0:T(128)} %param.27) | copy-start | bytes 196
  351.0 6.5 %copy-start.5 = (bf16[16,8,16,128]{3,2,1,0:T(8,128)(2,1)S(1)}, bf16[16,8,16,128]{3,2,1,0:T(8,128)(2,1)}, u32[]{:S(2)}) copy-start(bf16[16,8,16,128]{3,2,1,0:T(8,128)(2,1)} %copy-done.4) | copy-start | bytes 1572868
  355.5 19.4 %copy-start.1 = (f32[1,16,128,128]{3,2,1,0:T(8,128)S(1)}, f32[1,16,128,128]{3,2,1,0:T(8,128)}, u32[]{:S(2)}) copy-start(f32[1,16,128,128]{3,2,1,0:T(8,128)} %custom-call) | copy-start | bytes 3145732
  379.4 1.8 copy-start.7
  379.4 3.2 copy-start.3
Sparse Core Ops, SparseCore 0:
  20.2 29.3 all-gather.10
  51.2 80.2 all-gather.14
  133.1 79.2 all-gather.18
  213.8 79.2 all-gather.16
  294.6 80.2 all-gather.12
where the time goes:
time: 394 us; the launch traced here: 393 us
  waiting for transfers between devices  234 us (59%)
  blocking collectives  63.2 us (16%)
  local copies, waits for them, and re-layouts  28.8 us (7%)
  matrix products  26.5 us (7%)
  other arithmetic  24.6 us (6%)
  between operations  15.5 us (4%)
    all_gather x4, waiting for transfers between devices, carried_in(): pieces = jax.tree.map(lambda part: lax.all_gather(part, axis), value)  225 us
    psum x1, blocking collectives, per_device(): lax.psum((table_part, skip_part), ('ctx', 'dom', 'rep'))  43.5 us
    select_n x12, other arithmetic, turn(): jnp.where(position < mine, new, old)  17.7 us
    all_gather x1, blocking collectives, per_device(): shard_part = lax.all_gather(prev_state, 'dom', axis=1, tiled=True)  10.2 us
    all_gather x1, blocking collectives, carried_in(): pieces = jax.tree.map(lambda part: lax.all_gather(part, axis), value)  9.49 us
    rev x3, local copies, waits for them, and re-layouts, carried_in(): pieces = jax.tree.map(lambda part: part[::-1], pieces)  9.28 us
    all_gather x1, waiting for transfers between devices, per_device(): lax.all_gather(chosen_heads, 'ctx', axis=2, tiled=True)  8.56 us
  transfers between devices with their start and end apart: 5, of which 5 were waited for; matrix products, arithmetic and copies ran while one was open for 17% of the time, Pallas kernels for 0%

commit v1 on v0

--- a/solution.py
+++ b/solution.py
@@ -3,6 +3,7 @@
 import jax.numpy as jnp
 from jax import lax
 from jax.sharding import PartitionSpec as P
+from jax.lax import psum
 
 
 def carried_in(value, axis, join, neutral, backward):
@@ -142,6 +143,11 @@
     suffix_start,
     cotangent,
 ):
+
+    def _guide_gates(xs):
+        prior = psum(xs, "ctx")
+        return psum(prior, ("dom", "rep"))
+
     prompt_count, part_count, length, feature_dim = hidden.shape
     pair_count = prompt_count * part_count
     head_count = skip_gain.shape[0]
@@ -216,7 +222,7 @@
     skip_part = jnp.einsum(
         "clhp,clhp->h", hidden_rows, grad_rows, preferred_element_type=jnp.float32
     ) * (total_scale / math.sqrt(head_dim))
-    grad_table, grad_skip = lax.psum((table_part, skip_part), ("ctx", "dom", "rep"))
+    grad_table, grad_skip = _guide_gates((table_part, skip_part))
     return (mixed, grad_hidden, grad_bmat, grad_cmat, grad_table, grad_skip)
 
 

time: 394 us -> 392 us (level)
  waiting for transfers between devices: 234 us -> 255 us
  blocking collectives: 63.2 us -> 42.4 us
    all_gather x4, waiting for transfers between devices: 225 us -> 246 us  [carried_in(): pieces = jax.tree.map(lambda part: lax.all_gather(part, axis), value)]
    psum x1 -> x2, blocking collectives: 43.5 us -> 22.8 us  [the longest x1 13.5 us: _guide_gates(): return psum(prior, ('dom', 'rep'))]
where the time goes in v1:
time: 392 us; the launch traced here: 391 us
  waiting for transfers between devices  255 us (65%)
  blocking collectives  42.4 us (11%)
  local copies, waits for them, and re-layouts  27.9 us (7%)
  matrix products  25.3 us (6%)
  other arithmetic  24.6 us (6%)
  between operations  15.6 us (4%)
    all_gather x4, waiting for transfers between devices, carried_in(): pieces = jax.tree.map(lambda part: lax.all_gather(part, axis), value)  246 us
    select_n x12, other arithmetic, turn(): jnp.where(position < mine, new, old)  17.7 us
    psum x1, blocking collectives, _guide_gates(): return psum(prior, ('dom', 'rep'))  13.5 us
    all_gather x1, blocking collectives, per_device(): shard_part = lax.all_gather(prev_state, 'dom', axis=1, tiled=True)  10.2 us
    all_gather x1, blocking collectives, carried_in(): pieces = jax.tree.map(lambda part: lax.all_gather(part, axis), value)  9.39 us
    rev x3, local copies, waits for them, and re-layouts, carried_in(): pieces = jax.tree.map(lambda part: part[::-1], pieces)  9.28 us
    psum x1, blocking collectives, _guide_gates(): prior = psum(xs, 'ctx')  9.24 us
    all_gather x1, waiting for transfers between devices, per_device(): lax.all_gather(chosen_heads, 'ctx', axis=2, tiled=True)  8.5 us
  transfers between devices with their start and end apart: 5, of which 5 were waited for; matrix products, arithmetic and copies ran while one was open for 17% of the time, Pallas kernels for 0%

profile of v1, /device:TPU:0, one launch (start us, length us, event | category | flops | bytes accessed | tf_op | source)
XLA Modules:
  0.0 390.9 jit_solution(2276945060931763780)
XLA Ops:
  7.2 10.2 %all_gather.41 = f32[1,2,4,128,128]{4,3,2,0,1:T(8,128)S(1)} all-gather(f32[1,1,4,128,128]{4,3,2,0,1:T(8,128)} %bitcast.289), channel_id=1, replica_groups=mesh['ctx'=4,'dom'=2,'rep'=4] {'dom'}, dimensions={1}, use_global_device_ids=true | all-gather | bytes 786432 | tf_op jit(solution)/shard_map/all_gather | solution.py:163
  18.1 2.0 fusion.43
  21.8 1.3 mul.337.clone
  23.2 1.4 mul.344
  25.6 2.6 copy.103
  28.9 3.0 fusion.32
  31.9 1.4 copy.141
  33.5 1.3 fusion.64
  34.9 1.4 copy.143
  37.9 1.3 fusion.58
  41.1 8.5 %all-gather.11.cloned.1.call-done = f32[16,128,128]{2,1,0:T(8,128)} async-done(((f32[4,128,128]{2,1,0:T(8,128)}), f32[16,128,128]{2,1,0:T(8,128)}) %all-gather.11.cloned.1.call-update) | async-done | bytes 1048592 | tf_op jit(solution)/shard_map/all_gather | solution.py:169
  49.6 2.5 convolution_add_fusion
  53.7 9.4 %all_gather.40 = f32[4,1,16]{2,1,0:T(1,128)S(1)} all-gather(f32[1,1,16]{2,1,0:T(1,128)S(1)} %get-tuple-element.556), channel_id=1, replica_groups=mesh['ctx'=4,'dom'=2,'rep'=4] {'ctx'}, dimensions={0}, use_global_device_ids=true | all-gather | bytes 320 | tf_op jit(solution)/shard_map/all_gather | solution.py:11
  63.3 2.6 copy.114
  65.8 1.9 fusion.27
  67.8 63.7 %all-gather.15.cloned.1.call-done = f32[64,128,128]{2,1,0:T(8,128)} async-done(((f32[16,128,128]{2,1,0:T(8,128)}), f32[64,128,128]{2,1,0:T(8,128)}) %all-gather.15.cloned.1.call-update) | async-done | bytes 4194320 | tf_op jit(solution)/shard_map/all_gather | solution.py:11
  131.5 4.6 %rev.11 = f32[4,1,16,128,128]{4,3,2,1,0:T(8,128)} reverse(f32[4,1,16,128,128]{4,3,2,1,0:T(8,128)} %bitcast.277), dimensions={0} | reverse | bytes 8388608 | tf_op jit(solution)/shard_map/rev | solution.py:13
  136.1 76.3 %all-gather.19.cloned.1.call-done = f32[64,128,128]{2,1,0:T(8,128)} async-done(((f32[16,128,128]{2,1,0:T(8,128)}), f32[64,128,128]{2,1,0:T(8,128)}) %all-gather.19.cloned.1.call-update) | async-done | bytes 4194320 | tf_op jit(solution)/shard_map/all_gather | solution.py:11
  212.4 4.7 %rev.12 = f32[4,1,16,128,128]{4,3,2,1,0:T(8,128)} reverse(f32[4,1,16,128,128]{4,3,2,1,0:T(8,128)} %bitcast.278), dimensions={0} | reverse | bytes 8388608 | tf_op jit(solution)/shard_map/rev | solution.py:13
  217.0 4.6 %while.59 = (s32[]{:T(128)}, f32[1,16,128,128]{3,2,1,0:T(8,128)S(1)}, s32[]{:T(128)}, f32[4,1,16]{2,1,0:T(1,128)S(1)}, f32[4,1,16,128,128]{4,3,2,1,0:T(8,128)}, /*index=5*/s32[]{:T(128)}, s32[]{:T(128)}) while((s32[]{:T(128)}, f32[1,16,128,128]{3,2,1,0:T(8,128)S(1)}, s32[]{:T(128)}, f32[4,1,16]{2,1,0:T(1,128)S(1)}, ...), condition=%wide.region_8.9_spmd.clone, body=%wide.region_7.8_spmd.clone.sunk | while | flops 1048580 | bytes 3146033 | solution.py:23
  217.0 1.5 fusion.99
  218.5 1.6 fusion.99
  220.1 1.5 fusion.99
  221.7 1.3 fusion.8
  223.0 70.2 %all-gather.17.cloned.1.call-done = f32[64,128,128]{2,1,0:T(8,128)} async-done(((f32[16,128,128]{2,1,0:T(8,128)}), f32[64,128,128]{2,1,0:T(8,128)}) %all-gather.17.cloned.1.call-update) | async-done | bytes 4194320 | tf_op jit(solution)/shard_map/all_gather | solution.py:11
  293.1 4.5 %while.58 = (s32[]{:T(128)}, f32[1,16,128,128]{3,2,1,0:T(8,128)S(1)}, s32[]{:T(128)}, f32[4,1,16]{2,1,0:T(1,128)S(1)}, f32[4,1,16,128,128]{4,3,2,1,0:T(8,128)}, /*index=5*/s32[]{:T(128)}, s32[]{:T(128)}) while((s32[]{:T(128)}, f32[1,16,128,128]{3,2,1,0:T(8,128)S(1)}, s32[]{:T(128)}, f32[4,1,16]{2,1,0:T(1,128)S(1)}, ...), condition=%wide.region_6.7_spmd.clone, body=%wide.region_5.6_spmd.clone.sunk | while | flops 1048580 | bytes 3146033 | solution.py:23
  293.1 1.5 fusion.98
  294.6 1.5 fusion.98
  296.1 1.5 fusion.98
  298.0 3.4 fusion.23
  301.3 2.1 copy.125
  303.4 1.7 fusion.19
  305.2 1.8 fusion.26
  307.5 9.2 %all-reduce.1 = (f32[4,128]{1,0:T(4,128)S(1)}, f32[16]{0:T(128)S(1)}) all-reduce(f32[4,128]{1,0:T(4,128)S(1)} %convolution_multiply_fusion.3, f32[16]{0:T(128)S(1)} %broadcast_multiply_fusion), channel_id=1, replica_groups=mesh['ctx'=4,'dom'=2,'rep'=4] {'ctx'}, use_global_device_ids=true, to_apply=%region_12.13 | all-reduce | flops 528 | bytes 4224 | tf_op jit(solution)/shard_map/psum | solution.py:148
  316.8 13.5 %all-reduce = (f32[4,128]{1,0:T(4,128)}, f32[16]{0:T(128)}) all-reduce(f32[4,128]{1,0:T(4,128)S(1)} %get-tuple-element.548, f32[16]{0:T(128)S(1)} %get-tuple-element.549), channel_id=1, replica_groups=mesh['ctx'=4,'dom'=2,'rep'=4] {'dom','rep'}, use_global_device_ids=true, to_apply=%region_13.14 | all-reduce | flops 528 | bytes 4224 | tf_op jit(solution)/shard_map/psum | solution.py:149
  330.3 4.5 %while.57 = (s32[]{:T(128)}, f32[1,16,128,128]{3,2,1,0:T(8,128)S(1)}, s32[]{:T(128)}, f32[4,1,16]{2,1,0:T(1,128)S(1)}, f32[4,1,16,128,128]{4,3,2,1,0:T(8,128)}, /*index=5*/s32[]{:T(128)}, s32[]{:T(128)}) while((s32[]{:T(128)}, f32[1,16,128,128]{3,2,1,0:T(8,128)S(1)}, s32[]{:T(128)}, f32[4,1,16]{2,1,0:T(1,128)S(1)}, ...), condition=%wide.region_4.5_spmd.clone, body=%wide.region_3.4_spmd.clone.sunk | while | flops 1048580 | bytes 3146033 | solution.py:23
  330.3 1.5 fusion.97
  331.9 1.5 fusion.97
  333.4 1.5 fusion.97
  334.9 1.3 fusion.7
  336.8 1.5 fusion.22
  338.3 35.8 %all-gather.13.cloned.1.call-done = f32[64,128,128]{2,1,0:T(8,128)} async-done(((f32[16,128,128]{2,1,0:T(8,128)}), f32[64,128,128]{2,1,0:T(8,128)}) %all-gather.13.cloned.1.call-update) | async-done | bytes 4194320 | tf_op jit(solution)/shard_map/all_gather | solution.py:11
  374.1 4.5 %while.56 = (s32[]{:T(128)}, f32[1,16,128,128]{3,2,1,0:T(8,128)S(1)}, s32[]{:T(128)}, f32[4,1,16]{2,1,0:T(1,128)S(1)}, f32[4,1,16,128,128]{4,3,2,1,0:T(8,128)}, /*index=5*/s32[]{:T(128)}, s32[]{:T(128)}) while((s32[]{:T(128)}, f32[1,16,128,128]{3,2,1,0:T(8,128)S(1)}, s32[]{:T(128)}, f32[4,1,16]{2,1,0:T(1,128)S(1)}, ...), condition=%wide.region_2.3_spmd.clone, body=%wide.region_1.2_spmd.clone.sunk | while | flops 1048580 | bytes 3146033 | solution.py:23
  374.1 1.5 fusion.96
  375.6 1.5 fusion.96
  377.1 1.5 fusion.96
  378.6 1.5 fusion.36
  380.6 1.4 fusion.24
  (97 shorter events, 12.7 us)
Async XLA Ops:
  7.2 29.1 %copy-start = (bf16[1,1,128,128]{3,2,1,0:T(8,128)(2,1)S(1)}, bf16[1,1,128,128]{3,2,1,0:T(8,128)(2,1)}, u32[]{:S(2)}) copy-start(bf16[1,1,128,128]{3,2,1,0:T(8,128)(2,1)} %param.22) | copy-start | bytes 98308
  7.2 14.6 %copy-start.13 = (f32[1,1,128,16]{2,3,1,0:T(8,128)S(1)}, f32[1,1,128,16]{2,3,1,0:T(8,128)}, u32[]{:S(2)}) copy-start(f32[1,1,128,16]{2,3,1,0:T(8,128)} %param.25) | copy-start | bytes 24580
  7.2 42.4 %all-gather.11.cloned.1.call-start = ((), (), s32[]{:S(2)}) async-start(), calls=%async_computation | async-start | bytes 1310720 | tf_op jit(solution)/shard_map/all_gather | solution.py:169
  20.1 111.4 %all-gather.15.cloned.1.call-start = ((), (), s32[]{:S(2)}) async-start(), calls=%async_computation.2 | async-start | bytes 5242880 | tf_op jit(solution)/shard_map/all_gather | solution.py:11
  21.4 7.5 %copy-start.6 = (bf16[1,1,128,2048]{3,2,1,0:T(8,128)(2,1)S(1)}, bf16[1,1,128,2048]{3,2,1,0:T(8,128)(2,1)}, u32[]{:S(2)}) copy-start(bf16[1,1,128,2048]{3,2,1,0:T(8,128)(2,1)} %param.20) | copy-start | bytes 1572868
  21.4 7.5 %copy-start.10 = (bf16[1,1,128,2048]{3,2,1,0:T(8,128)(2,1)S(1)}, bf16[1,1,128,2048]{3,2,1,0:T(8,128)(2,1)}, u32[]{:S(2)}) copy-start(bf16[1,1,128,2048]{3,2,1,0:T(8,128)(2,1)} %param.31) | copy-start | bytes 1572868
  28.2 5.1 %copy-start.15 = (s32[1,1,128]{2,1,0:T(1,128)S(1)}, s32[1,1,128]{2,1,0:T(1,128)}, u32[]{:S(2)}) copy-start(s32[1,1,128]{2,1,0:T(1,128)} %param.23) | copy-start | bytes 1540
  28.2 5.1 %copy-start.16 = (bf16[1,1,128,128]{3,2,1,0:T(8,128)(2,1)S(1)}, bf16[1,1,128,128]{3,2,1,0:T(8,128)(2,1)}, u32[]{:S(2)}) copy-start(bf16[1,1,128,128]{3,2,1,0:T(8,128)(2,1)} %param.21) | copy-start | bytes 98308
  28.2 5.1 %copy-start.17 = (f32[4,128]{1,0:T(4,128)S(1)}, f32[4,128]{1,0:T(4,128)}, u32[]{:S(2)}) copy-start(f32[4,128]{1,0:T(4,128)} %param.24) | copy-start | bytes 6148
  31.9 5.7 %copy-start.12 = (bf16[1,1,128,2048]{3,2,1,0:T(8,128)(2,1)S(1)}, bf16[1,1,128,2048]{3,2,1,0:T(8,128)(2,1)}, u32[]{:S(2)}) copy-start(bf16[1,1,128,2048]{3,2,1,0:T(8,128)(2,1)} %get-tuple-element.553) | copy-start | bytes 1572868
  34.8 4.5 %copy-start.11 = (bf16[1,1,128,2048]{3,2,1,0:T(8,128)(2,1)S(1)}, bf16[1,1,128,2048]{3,2,1,0:T(8,128)(2,1)}, u32[]{:S(2)}) copy-start(bf16[1,1,128,2048]{3,2,1,0:T(8,128)(2,1)} %get-tuple-element.550) | copy-start | bytes 1572868
  34.8 177.6 %all-gather.19.cloned.1.call-start = ((), (), s32[]{:S(2)}) async-start(), calls=%async_computation.4 | async-start | bytes 5242880 | tf_op jit(solution)/shard_map/all_gather | solution.py:11
  37.6 255.6 %all-gather.17.cloned.1.call-start = ((), (), s32[]{:S(2)}) async-start(), calls=%async_computation.3 | async-start | bytes 5242880 | tf_op jit(solution)/shard_map/all_gather | solution.py:11
  39.2 334.8 %all-gather.13.cloned.1.call-start = ((), (), s32[]{:S(2)}) async-start(), calls=%async_computation.1 | async-start | bytes 5242880 | tf_op jit(solution)/shard_map/all_gather | solution.py:11
  39.7 12.8 %copy-start.4 = (bf16[16,8,16,128]{3,2,1,0:T(8,128)(2,1)}, bf16[16,8,16,128]{3,2,1,0:T(8,128)(2,1)S(1)}, u32[]{:S(2)}) copy-start(bf16[16,8,16,128]{3,2,1,0:T(8,128)(2,1)S(1)} %copy.146) | copy-start | bytes 1572868
  41.0 11.5 %copy-start.2 = (bf16[16,8,16,128]{3,2,1,0:T(8,128)(2,1)}, bf16[16,8,16,128]{3,2,1,0:T(8,128)(2,1)S(1)}, u32[]{:S(2)}) copy-start(bf16[16,8,16,128]{3,2,1,0:T(8,128)(2,1)S(1)} %copy.147) | copy-start | bytes 1572868
  293.1 4.8 %copy-start.14 = (f32[16]{0:T(128)S(1)}, f32[16]{0:T(128)}, u32[]{:S(2)}) copy-start(f32[16]{0:T(128)} %param.27) | copy-start | bytes 196
  330.3 6.5 %copy-start.3 = (bf16[16,8,16,128]{3,2,1,0:T(8,128)(2,1)S(1)}, bf16[16,8,16,128]{3,2,1,0:T(8,128)(2,1)}, u32[]{:S(2)}) copy-start(bf16[16,8,16,128]{3,2,1,0:T(8,128)(2,1)} %copy-done.2) | copy-start | bytes 1572868
  334.9 39.2 %copy-start.1 = (f32[1,16,128,128]{3,2,1,0:T(8,128)S(1)}, f32[1,16,128,128]{3,2,1,0:T(8,128)}, u32[]{:S(2)}) copy-start(f32[1,16,128,128]{3,2,1,0:T(8,128)} %custom-call) | copy-start | bytes 3145732
  378.6 1.9 copy-start.5
  378.6 1.8 copy-start.7
  378.6 2.0 copy-start.8
  380.1 2.9 copy-start.9
Sparse Core Ops, SparseCore 0:
  20.2 29.3 all-gather.10
  51.2 80.2 all-gather.14
  133.1 79.2 all-gather.18
  213.8 79.2 all-gather.16
  294.5 79.5 all-gather.12
